TPU v7x, 32 devices: a whole 2x2x4 slice. The times are simulated.
32 devices in a mesh: grp: 2 (over y), mem: 8 (over z, x), slab: 2 (over core).
Axes of the slice: x: 2, y: 2, z: 4, core: 2. Of those that a mesh axis runs over, the one named last changes fastest.
Arguments:
- parameter_field: float32 [32, 32, 32, 256], P(('grp', 'mem'), 'slab'), parts along dimension 0, may hold values from -5 to 5
- initial_tracer: float32 [64, 32, 256], P(('grp', 'slab')), parts along dimension 0, may hold values from -1 to 1
- observed: float32 [8192], P(('grp', 'slab')), parts along dimension 0, may hold values from -3 to 3
- observation_variance: float32 [8192], P(('grp', 'slab')), parts along dimension 0, may hold values from 0.25 to 2.5
- observation_index: int32 [8192], P(('grp', 'slab')), parts along dimension 0, may hold values from 0 to 262143, as said below
- noise: float32 [32, 16], P('grp'), parts along dimension 0, may hold values from -6 to 6
Outputs:
- new_field: float32 [32, 32, 32, 256], P(('grp', 'mem'), 'slab'), parts along dimension 0
- predicted: float32 [32, 4096], P(('grp', 'mem'), 'slab'), parts along dimension 0
- mixing: float32 [32, 16], P(('grp', 'mem')), parts along dimension 0
There are 2 independent parts, one for each index of `grp`. A program takes and returns all parts, laid end to end along the dimension named above; each array names one. Nothing has to cross between parts.
Inputs may be any that keep to these rules, and one draw needn't show every extreme that they name: `observation_index`: observation i names a flattened cell whose x lies in x-slab i // 2048, that is from (i // 2048) * 16 to (i // 2048) * 16 + 15; cells may repeat.
All inputs are finite; a program needn't handle non-finite values.
Results may differ from a plain program's by a relative error of at most 0.00011.
Values sent between devices are 32-bit elements; how exact they have to be, the bound alone decides.
No kernel may reach another device: no remote copies, remote signals or barrier semaphores. Data moves between devices by JAX's collectives and lax.ppermute only.
A program may use at most 192 MiB of HBM per device.

v0:
```python
import functools

import jax
import jax.numpy as jnp
from jax import lax
from jax.experimental import pallas as pl
from jax.experimental.pallas import tpu as pltpu
from jax.sharding import PartitionSpec as P


STEPS = 3

ADVECT_SPEED = 0.1
KAPPA_BASE = 0.07
KAPPA_SWING = 0.05
STEP_SCALE = 0.02
PRIOR_VARIANCE = 0.02
EPSILON = 1e-06

LANES = 128
SUBLANES = 8

VMEM = pl.BlockSpec(memory_space=pltpu.VMEM)
SMEM = pl.BlockSpec(memory_space=pltpu.SMEM)
SMALL = pltpu.CompilerParams(vmem_limit_bytes=20 * 2**20)


def ring(axis):
    count = lax.axis_size(axis)
    forward = [(i, (i + 1) % count) for i in range(count)]
    backward = [(target, source) for source, target in forward]
    return forward, backward


def twice_flux(left, right):
    speed = jnp.maximum(jnp.abs(left), jnp.abs(right))
    return (left * left + right * right) - (speed + speed) * (right - left)


def level_shifts(center, row):
    count = center.shape[0] // SUBLANES
    tiles = [center[t * SUBLANES : (t + 1) * SUBLANES] for t in range(count)]
    down = [pltpu.roll(tile, SUBLANES - 1, 0) for tile in tiles]
    up = [pltpu.roll(tile, 1, 0) for tile in tiles]
    upper = [
        jnp.where(row == SUBLANES - 1, down[t + 1] if t + 1 < count else tiles[t], down[t])
        for t in range(count)
    ]
    lower = [jnp.where(row == 0, up[t - 1] if t else tiles[t], up[t]) for t in range(count)]
    return jnp.concatenate(upper, axis=0), jnp.concatenate(lower, axis=0)


def laplacian(below, center, above, row):
    columns = center.shape[1]
    upper, lower = level_shifts(center, row)
    return (
        above
        + below
        + upper
        + lower
        + pltpu.roll(center, 1, 1)
        + pltpu.roll(center, columns - 1, 1)
        - 6.0 * center
    )


def sweep(count, body, flux):
    if count % 2:
        return lax.fori_loop(0, count, body, flux)
    return lax.fori_loop(0, count // 2, lambda i, f: body(2 * i + 1, body(2 * i, f)), flux)


def forward_kernel(
    line_ref,
    index_ref,
    tracer_ref,
    param_ref,
    below_ref,
    above_ref,
    low_ref,
    high_ref,
    observed_ref,
    variance_ref,
    out_ref,
    seen_ref,
    target_ref,
    weight_ref,
    ext,
    kappa,
    buf_a,
    buf_b,
    table,
    stage,
):
    members, width, levels, columns = param_ref.shape
    rim = STEPS - 1
    halves = columns // LANES
    pitch = SUBLANES
    row = lax.broadcasted_iota(jnp.int32, (SUBLANES, columns), 0)

    target_ref[...] = observed_ref[...]
    weight_ref[...] = variance_ref[...]
    for i in range(STEPS):
        ext[i] = below_ref[below_ref.shape[0] - STEPS + i]
        ext[STEPS + width + i] = above_ref[i]

    @pl.loop(0, width)
    def _(i):
        ext[STEPS + i] = tracer_ref[i]
        for m in range(members):
            kappa[m, rim + i] = KAPPA_BASE + KAPPA_SWING * jnp.tanh(param_ref[m, i])

    for m in range(members):
        for i in range(rim):
            kappa[m, i] = KAPPA_BASE + KAPPA_SWING * jnp.tanh(low_ref[m, i])
            kappa[m, rim + width + i] = KAPPA_BASE + KAPPA_SWING * jnp.tanh(high_ref[m, i])

    def step_first(i, flux_low):
        center, above = ext[i + 1], ext[i + 2]
        flux_high = twice_flux(center, above)
        lap = laplacian(ext[i], center, above, row)
        base = center - (0.25 * ADVECT_SPEED) * (flux_high - flux_low)
        for m in range(members):
            buf_a[m, i] = base + kappa[m, i] * lap
        return flux_high

    sweep(width + 2 * rim, step_first, twice_flux(ext[0], ext[1]))

    for number in range(1, STEPS):
        source, target = (buf_a, buf_b) if number % 2 else (buf_b, buf_a)
        margin = STEPS - 1 - number
        last = number == STEPS - 1
        for m in range(members):

            def step_next(i, flux_low):
                center, above = source[m, i + 1], source[m, i + 2]
                flux_high = twice_flux(center, above)
                lap = laplacian(source[m, i], center, above, row)
                new = (
                    center
                    - (0.25 * ADVECT_SPEED) * (flux_high - flux_low)
                    + kappa[m, i + number] * lap
                )
                if last:
                    for h in range(halves):
                        at = i * (levels * halves * pitch) + h * pitch + m
                        table[pl.ds(at, levels, stride=halves * pitch), :] = new[
                            :, h * LANES : (h + 1) * LANES
                        ]
                else:
                    target[m, i] = new
                return flux_high

            sweep(width + 2 * margin, step_next, twice_flux(source[m, 0], source[m, 1]))

    sublane = lax.broadcasted_iota(jnp.int32, (LANES, LANES), 0)
    groups = out_ref.shape[1] // LANES

    for group in range(groups):
        first = group * LANES
        base = group % 2 * members * LANES
        for o in range(LANES):
            at = pl.multiple_of(line_ref[first + o], pitch)
            stage[base + o * members : base + (o + 1) * members, :] = table[
                pl.ds(at, members), :
            ]
        wanted = sublane == (index_ref[group : group + 1, :] & (LANES - 1))
        for m in range(members):
            turned = stage[pl.ds(base + m, LANES, stride=members), :].T
            picked = jnp.sum(jnp.where(wanted, turned, 0.0), axis=0, keepdims=True)
            out_ref[m : m + 1, first : first + LANES] = picked
            seen_ref[0, m * groups + group : m * groups + group + 1, :] = picked
    for b in range(1, seen_ref.shape[0]):
        seen_ref[b] = seen_ref[0]


def forward_observe(index, tracer, param, layers, params, observed, variance, copies=1):
    members, width, levels, columns = param.shape
    count = index.shape[0]
    rim = STEPS - 1
    rows = width * levels * (columns // LANES) * SUBLANES
    cell = index - lax.axis_index("slab") * (width * levels * columns)
    return pl.pallas_call(
        forward_kernel,
        out_shape=(
            jax.ShapeDtypeStruct((members, count), jnp.float32),
            jax.ShapeDtypeStruct((copies, members * count // LANES, LANES), jnp.float32),
            jax.ShapeDtypeStruct((count // LANES, LANES), jnp.float32),
            jax.ShapeDtypeStruct((count // LANES, LANES), jnp.float32),
        ),
        in_specs=[SMEM] + [VMEM] * 9,
        out_specs=(VMEM,) * 4,
        scratch_shapes=[
            pltpu.VMEM((width + 2 * STEPS, levels, columns), jnp.float32),
            pltpu.VMEM((members, width + 2 * rim, levels, columns), jnp.float32),
            pltpu.VMEM((members, width + 2 * rim, levels, columns), jnp.float32),
            pltpu.VMEM((members, width + 2 * rim, levels, columns), jnp.float32),
            pltpu.VMEM((rows, LANES), jnp.float32),
            pltpu.VMEM((2 * members * LANES, LANES), jnp.float32),
        ],
        cost_estimate=pl.CostEstimate(
            flops=100 * param.size, bytes_accessed=16 * param.size, transcendentals=param.size
        ),
        compiler_params=SMALL,
        name="forward_observe",
    )(
        lax.shift_right_logical(cell, 7) * SUBLANES,
        index.reshape(-1, LANES),
        tracer,
        param,
        *layers,
        *params,
        observed.reshape(-1, LANES),
        variance.reshape(-1, LANES),
    )


def gram_kernel(order, *refs):
    owners = len(order)
    blocks = refs[:owners]
    dev_ref, mean_ref, packed_ref = refs[owners:]
    members, rows, columns = blocks[0].shape
    ensemble = owners * members
    me = lax.axis_index("mem")

    @pl.loop(0, rows // SUBLANES)
    def _(r):
        at = pl.ds(pl.multiple_of(r * SUBLANES, SUBLANES), SUBLANES)
        parts = [blocks[b][m, at, :] for b in range(owners) for m in range(members)]
        total = parts[0]
        for part in parts[1:]:
            total = total + part
        mean = total * (1.0 / ensemble)
        mean_ref[at, :] = mean
        for i, b in enumerate(order):
            for m in range(members):
                dev_ref[(me ^ b) * members + m, at, :] = parts[i * members + m] - mean

    row = lax.broadcasted_iota(jnp.int32, (SUBLANES, LANES), 0)
    lane = lax.broadcasted_iota(jnp.int32, (SUBLANES, LANES), 1)

    def fold(left, right):
        product = left * right
        while product.shape[0] > SUBLANES:
            cut = product.shape[0] // 2
            product = product[:cut] + product[cut:]
        total = product[:, :LANES]
        for h in range(1, columns // LANES):
            total = total + product[:, h * LANES : (h + 1) * LANES]
        return jnp.sum(total, axis=0, keepdims=True)

    tiles = range(0, ensemble, SUBLANES)
    upper = [jnp.zeros((SUBLANES, LANES), jnp.float32) for _ in tiles]
    shifts = [jnp.zeros((SUBLANES, LANES), jnp.float32) for _ in tiles]
    means = mean_ref[...]
    for k in range(ensemble):
        left = dev_ref[k]
        shift = fold(left, means)
        shifts[k // SUBLANES] = jnp.where(row == k % SUBLANES, shift, shifts[k // SUBLANES])
        sums = [fold(left, dev_ref[j]) for j in range(k + 1)]
        for t, first in enumerate(tiles):
            stack = None
            for j in range(first, min(first + SUBLANES, k + 1)):
                stack = sums[j] if stack is None else jnp.where(row == j - first, sums[j], stack)
            if stack is not None:
                column = jnp.sum(jnp.broadcast_to(stack, row.shape), axis=1, keepdims=True)
                upper[t] = jnp.where(lane == k, column, upper[t])
    number = lax.broadcasted_iota(jnp.int32, (ensemble, LANES), 0)
    position = lax.broadcasted_iota(jnp.int32, (ensemble, LANES), 1)
    whole = jnp.where(position >= number, jnp.concatenate(upper, axis=0), 0.0)
    square = jnp.concatenate([whole, jnp.zeros((LANES - ensemble, LANES), jnp.float32)], axis=0)
    mirrored = jnp.where(position < number, square.T[:ensemble], whole)
    mirrored = mirrored + jnp.sum(jnp.concatenate(shifts, axis=0), axis=1, keepdims=True)
    packed = jnp.zeros((SUBLANES, LANES), jnp.float32)
    for t, first in enumerate(tiles):
        part = pltpu.roll(mirrored[first : first + SUBLANES], t * ensemble, 1)
        inside = (lane >= t * ensemble) & (lane < (t + 1) * ensemble)
        packed = jnp.where(inside, part, packed)
    packed_ref[...] = packed


def gram_call(blocks, order):
    owners = len(order)
    members, rows, columns = blocks[0].shape
    ensemble = owners * members
    return pl.pallas_call(
        functools.partial(gram_kernel, order),
        out_shape=(
            jax.ShapeDtypeStruct((ensemble, rows, columns), jnp.float32),
            jax.ShapeDtypeStruct((rows, columns), jnp.float32),
            jax.ShapeDtypeStruct((SUBLANES, LANES), jnp.float32),
        ),
        in_specs=[VMEM] * owners,
        out_specs=(VMEM,) * 3,
        compiler_params=SMALL,
        name="prior_products",
    )(*blocks)


def send_kernel(prior_ref, data_ref, load_ref):
    total = prior_ref[...] + data_ref[...]
    for i in range(load_ref.shape[0]):
        load_ref[i] = total


def send_call(prior, data, copies):
    return pl.pallas_call(
        send_kernel,
        out_shape=jax.ShapeDtypeStruct((copies,) + prior.shape, jnp.float32),
        in_specs=[VMEM] * 2,
        out_specs=VMEM,
        compiler_params=SMALL,
        name="send_products",
    )(prior, data)


def pack_products(part):
    count = part.shape[0]
    halves = [part[t : t + SUBLANES] for t in range(0, count, SUBLANES)]
    wide = jnp.concatenate(halves, axis=1)
    return jnp.pad(wide, ((0, 0), (LANES // 2, LANES // 2 - wide.shape[1])))


def mix_kernel(
    total_cells, order, sums_ref, noise_ref, dev_ref, mean_ref, *refs
):
    outs = refs[: len(order)]
    rows_ref, coef = refs[len(order) :]
    ensemble, rows, columns = dev_ref.shape
    members = outs[0].shape[0]
    me = lax.axis_index("mem")

    packed = sums_ref[0]
    for i in range(1, sums_ref.shape[0]):
        packed = packed + sums_ref[i]

    def unpack(first):
        parts = [
            packed[:, first + t * ensemble : first + (t + 1) * ensemble]
            for t in range(ensemble // SUBLANES)
        ]
        return jnp.concatenate(parts, axis=0)

    data_gram = unpack(LANES // 2) * (1.0 / ensemble)
    prior_gram = unpack(0) * (1.0 / (ensemble * PRIOR_VARIANCE * total_cells))
    power = jnp.sum(data_gram * data_gram, keepdims=True) / (ensemble * ensemble)
    step_size = STEP_SCALE / jnp.sqrt(power + EPSILON)
    mixing = (
        -step_size * (data_gram + prior_gram)
        + jnp.sqrt(2.0 * step_size / ensemble) * noise_ref[...]
    )
    rows_ref[...] = mixing
    weight = mixing + jnp.where(
        lax.broadcasted_iota(jnp.int32, mixing.shape, 0)
        == lax.broadcasted_iota(jnp.int32, mixing.shape, 1),
        1.0,
        0.0,
    )
    for j in range(ensemble):
        coef[j] = jnp.broadcast_to(weight[:, j : j + 1], (ensemble, LANES))

    for out, b in zip(outs, order):
        for m in range(members):
            j = (me ^ b) * members + m

            @pl.loop(0, rows // (2 * SUBLANES))
            def _(r):
                at = pl.ds(pl.multiple_of(r * 2 * SUBLANES, 2 * SUBLANES), 2 * SUBLANES)
                total = mean_ref[at, :]
                for k in range(ensemble):
                    scale = jnp.broadcast_to(coef[j, k : k + 1, :], (2 * SUBLANES, LANES))
                    scale = jnp.concatenate([scale] * (columns // LANES), axis=1)
                    total = total + scale * dev_ref[k, at, :]
                out[m, at, :] = total


def mix_call(sums, noise, dev, mean, total_cells, order):
    ensemble, rows, columns = dev.shape
    members = ensemble // lax.axis_size("mem")
    block = jax.ShapeDtypeStruct((members, rows, columns), jnp.float32)
    result = pl.pallas_call(
        functools.partial(mix_kernel, total_cells, order),
        out_shape=(block,) * len(order)
        + (jax.ShapeDtypeStruct((ensemble, ensemble), jnp.float32),),
        in_specs=[VMEM] * 4,
        out_specs=(VMEM,) * (len(order) + 1),
        scratch_shapes=[pltpu.VMEM((ensemble, ensemble, LANES), jnp.float32)],
        compiler_params=SMALL,
        name="mix_update",
    )(sums, noise, dev, mean)
    return result[:-1], result[-1]


def cut_blocks(param, owners):
    members, width, levels, columns = param.shape
    flat = param.reshape(members, width * levels, columns)
    rows = width * levels // owners
    me = lax.axis_index("mem")
    return [
        lax.dynamic_slice_in_dim(flat, (me ^ b) * rows, rows, axis=1) for b in range(owners)
    ]


def slab_rims(tracer, param):
    rim = STEPS - 1
    forward, backward = ring("slab")
    if set(forward) == set(backward):
        moved = lax.ppermute(tracer, "slab", forward)
        layers = (moved, moved)
    else:
        layers = (
            lax.ppermute(tracer[-STEPS:], "slab", forward),
            lax.ppermute(tracer[:STEPS], "slab", backward),
        )
    params = (
        lax.ppermute(param[:, -rim:], "slab", forward),
        lax.ppermute(param[:, :rim], "slab", backward),
    )
    return layers, params


def join_kernel(order, *refs):
    owners = len(order)
    blocks = refs[:owners]
    out_ref, sem = refs[owners:]
    me = lax.axis_index("mem")
    rows = blocks[0].shape[1]
    started = []
    for i, b in enumerate(order):
        at = pl.ds(pl.multiple_of((me ^ b) * rows, rows), rows)
        started.append(pltpu.make_async_copy(blocks[i], out_ref.at[:, at], sem.at[i]))
    for copy in started:
        copy.start()
    for copy in started:
        copy.wait()


def join_call(blocks, order):
    owners = len(blocks)
    members, rows, columns = blocks[0].shape
    return pl.pallas_call(
        functools.partial(join_kernel, order),
        out_shape=jax.ShapeDtypeStruct((members, owners * rows, columns), jnp.float32),
        in_specs=[VMEM] * owners,
        out_specs=pl.BlockSpec(memory_space=pl.ANY),
        scratch_shapes=[pltpu.SemaphoreType.DMA((owners,))],
        compiler_params=SMALL,
        name="join_blocks",
    )(*blocks)


def dot32(spec, a, b):
    return jnp.einsum(
        spec, a, b, precision=lax.Precision.HIGHEST, preferred_element_type=jnp.float32
    )


def far_first(owners):
    half = owners // 2
    return (1,) + tuple(range(owners - 1, half - 1, -1)) + tuple(range(half - 1, 1, -1)) + (0,)


def swap(block, b):
    count = lax.axis_size("mem")
    return lax.ppermute(block, "mem", [(i, i ^ b) for i in range(count)])


def data_products(values, observed, variance):
    spread = values - jnp.mean(values, axis=0, keepdims=True)
    weighted = (values - observed[None]) / variance[None]
    return dot32("ko,jo->kj", spread, weighted)


def broadcast_exchange(load, axes):
    return lax.all_to_all(load, axes, split_axis=0, concat_axis=0, tiled=True)


def small_ensemble(
    parameter_field, initial_tracer, observed, observation_variance, observation_index, noise
):
    members_here, slab_width, levels, columns = parameter_field.shape
    ensemble = noise.shape[0]
    owners = lax.axis_size("mem")
    total_cells = slab_width * levels * columns * lax.axis_size("slab")

    slabs = lax.axis_size("slab")
    blocks = cut_blocks(parameter_field, owners)
    order = far_first(owners)
    layers, params = slab_rims(initial_tracer, parameter_field)
    near = []
    for b in order[:-1]:
        near.append(swap(blocks[b], b))
    near.append(blocks[0])
    predicted, seen, target, spread = forward_observe(
        observation_index,
        initial_tracer,
        parameter_field,
        layers,
        params,
        observed,
        observation_variance,
        owners,
    )
    values = broadcast_exchange(seen, "mem").reshape(ensemble, -1)
    data_part = data_products(values, target.reshape(-1), spread.reshape(-1))

    dev, mean, prior_part = gram_call(near, order)
    load = send_call(prior_part, pack_products(data_part / owners), owners * slabs)
    sums = broadcast_exchange(load, ("mem", "slab"))
    sent, mixing = mix_call(sums, noise, dev, mean, total_cells, order)
    back = [swap(block, b) for b, block in zip(order[:-1], sent)] + [sent[-1]]
    new_field = join_call(back, order).reshape(parameter_field.shape)
    mixing_rows = lax.dynamic_slice_in_dim(
        mixing, lax.axis_index("mem") * members_here, members_here, 0
    )
    return (new_field, predicted, mixing_rows)


def large_ensemble(
    parameter_field, initial_tracer, observed, observation_variance, observation_index, noise
):
    members_here, slab_width, levels, columns = parameter_field.shape
    ensemble = noise.shape[0]
    owners = lax.axis_size("mem")
    cell_rows = slab_width * levels
    rows = cell_rows // owners
    total_cells = cell_rows * columns * lax.axis_size("slab")
    layers, params = slab_rims(initial_tracer, parameter_field)
    blocks = parameter_field.reshape(members_here, owners, rows, columns).transpose(1, 0, 2, 3)
    near = lax.all_to_all(blocks, "mem", split_axis=0, concat_axis=0, tiled=True)
    predicted = forward_observe(
        observation_index,
        initial_tracer,
        parameter_field,
        layers,
        params,
        observed,
        observation_variance,
    )[0]
    flat = near.reshape(ensemble, rows * columns)
    deviation = flat - jnp.mean(flat, axis=0, keepdims=True)
    prior_part = dot32("kc,jc->kj", deviation, flat)

    values = lax.all_gather(predicted, "mem", axis=0, tiled=True)
    data_part = data_products(values, observed, observation_variance)
    data_gram = lax.psum(data_part, "slab") / ensemble
    prior_gram = lax.psum(prior_part, ("mem", "slab")) / (
        ensemble * PRIOR_VARIANCE * total_cells
    )
    step_size = STEP_SCALE / jnp.sqrt(jnp.mean(data_gram * data_gram) + EPSILON)
    mixing = -step_size * (data_gram + prior_gram) + jnp.sqrt(2.0 * step_size / ensemble) * noise
    updated = flat + dot32("kj,kc->jc", mixing, deviation)
    returned = lax.all_to_all(
        updated.reshape(owners, members_here, rows, columns),
        "mem",
        split_axis=0,
        concat_axis=0,
        tiled=True,
    )
    new_field = returned.transpose(1, 0, 2, 3).reshape(parameter_field.shape)
    mixing_rows = lax.dynamic_slice_in_dim(
        mixing, lax.axis_index("mem") * members_here, members_here, 0
    )
    return (new_field, predicted, mixing_rows)


def per_device(*arrays):
    owners = lax.axis_size("mem")
    ensemble = arrays[-1].shape[0]
    if is_small(owners, ensemble):
        return small_ensemble(*arrays)
    return large_ensemble(*arrays)


def is_small(owners, ensemble):
    swaps = owners > 1 and owners & (owners - 1) == 0 and ensemble % SUBLANES == 0
    return swaps and ensemble <= 2 * SUBLANES


def solution(mesh):
    in_specs = (
        P(("grp", "mem"), "slab", None, None),
        P(("grp", "slab"), None, None),
        P(("grp", "slab")),
        P(("grp", "slab")),
        P(("grp", "slab")),
        P("grp", None),
    )
    out_specs = (
        P(("grp", "mem"), "slab", None, None),
        P(("grp", "mem"), "slab"),
        P(("grp", "mem"), None),
    )
    return jax.shard_map(
        per_device, mesh=mesh, in_specs=in_specs, out_specs=out_specs, check_vma=False
    )
```

profile of v0, /device:TPU:0, one launch (start us, length us, event | category | flops | bytes accessed | tf_op | source)
XLA Modules:
  0.0 93.9 jit_solution(16133765984140702834)
XLA Ops:
  0.6 0.6 collective-permute-start.7
  1.2 1.7 %fusion.1 = (f32[2,2,32,256]{3,2,1,0:T(8,128)}, f32[2,2,32,256]{3,2,1,0:T(8,128)}) fusion(f32[2,16,32,256]{3,2,1,0:T(8,128)} %param_ref.1), kind=kLoop, calls=%fused_computation.18 | loop fusion | bytes 524288 | tf_op jit(solution)/shard_map/slice | solution.py:417
  2.9 0.0 collective-permute-start.9
  2.9 0.5 collective-permute-start.8
  3.4 2.2 %constant_dynamic-slice_fusion.1 = (f32[2,64,256]{2,1,0:T(8,128)S(1)}, f32[2,64,256]{2,1,0:T(8,128)}, f32[2,64,256]{2,1,0:T(8,128)}, f32[2,64,256]{2,1,0:T(8,128...) fusion(f32[2,512,256]{2,1,0:T(8,128)} %bitcast.12, ...), kind=kLoop, calls=%fused_computation.10 | loop fusion | bytes 2097184 | tf_op jit(solution)/shard_map/dynamic_slice | solution.py:400
  5.6 2.6 %collective-permute-start.6 = (f32[2,64,256]{2,1,0:T(8,128)}, f32[2,64,256]{2,1,0:T(8,128)S(1)}, u32[]{:S(2)}, u32[]{:S(2)}) collective-permute-start(f32[2,64,256]{2,1,0:T(8,128)} %get-tuple-element.38), channel_id=1, source_target_pairs={{0,4},{2,6},{4,0},{6,2},{8,12},{10,14},{12,8},{14,10},{1,5},{3,7},... | collective-permute-start | bytes 393224 | tf_op jit(solution)/shard_map/ppermute | solution.py:465
  8.2 1.4 %collective-permute-start.5 = (f32[2,64,256]{2,1,0:T(8,128)}, f32[2,64,256]{2,1,0:T(8,128)S(1)}, u32[]{:S(2)}, u32[]{:S(2)}) collective-permute-start(f32[2,64,256]{2,1,0:T(8,128)} %get-tuple-element.39), channel_id=1, source_target_pairs={{0,6},{2,4},{4,2},{6,0},{8,14},{10,12},{12,10},{14,8},{1,7},{3,5},... | collective-permute-start | bytes 393224 | tf_op jit(solution)/shard_map/ppermute | solution.py:465
  9.6 0.0 collective-permute-done.9.high_ref
  9.6 0.0 collective-permute-done.8.low_ref
  9.6 0.0 collective-permute-done.7.below_ref.above_ref
  9.6 0.6 copy-done.3
  10.2 0.0 copy-done.4
  10.3 8.5 %forward_observe.1 = (f32[2,2048]{1,0:T(2,128)}, f32[8,32,128]{2,1,0:T(8,128)}, f32[16,128]{1,0:T(8,128)S(1)}, f32[16,128]{1,0:T(8,128)S(1)}) custom-call(s32[2048]{0:T(1024)S(1)} %shift-right-logical_multiply_fusion.line_ref, s32[16,128]{1,0:T(8,128)S(1)} %bitcast.13, f32[16,32,256]{2,1,0:T(8,128)S(1)} %copy-done.1, f32[2,16,32,256]{3,2,1,0:T(8,128)S(1)} %copy-done, ...), custom_call_target="tpu_custom_call" | custom-call | flops 26214400 | bytes 4194304 | tf_op jit(solution)/shard_map/forward_observe/pallas_call | solution.py:183
  18.7 4.9 %all-to-all-start = ((f32[8,32,128]{2,1,0:T(8,128)}), f32[8,32,128]{2,1,0:T(8,128)S(1)}, u32[]{:S(2)}, u32[]{:S(2)}) async-start(f32[8,32,128]{2,1,0:T(8,128)} %get-tuple-element.20), calls=%async_computation | async-start | bytes 262144 | tf_op jit(solution)/shard_map/all_to_all | solution.py:475
  23.6 2.9 %collective-permute-start.4 = (f32[2,64,256]{2,1,0:T(8,128)S(1)}, f32[2,64,256]{2,1,0:T(8,128)S(1)}, u32[]{:S(2)}, u32[]{:S(2)}) collective-permute-start(f32[2,64,256]{2,1,0:T(8,128)S(1)} %get-tuple-element.40), channel_id=1, source_target_pairs={{0,8},{2,10},{4,12},{6,14},{8,0},{10,2},{12,4},{14,6},{1,9},{3,11}... | collective-permute-start | bytes 393224 | tf_op jit(solution)/shard_map/ppermute | solution.py:465
  26.5 1.5 %collective-permute-start.3 = (f32[2,64,256]{2,1,0:T(8,128)S(1)}, f32[2,64,256]{2,1,0:T(8,128)S(1)}, u32[]{:S(2)}, u32[]{:S(2)}) collective-permute-start(f32[2,64,256]{2,1,0:T(8,128)S(1)} %get-tuple-element.41), channel_id=1, source_target_pairs={{0,10},{2,8},{4,14},{6,12},{8,2},{10,0},{12,6},{14,4},{1,11},{3,9}... | collective-permute-start | bytes 393224 | tf_op jit(solution)/shard_map/ppermute | solution.py:465
  28.0 3.3 %collective-permute-start.2 = (f32[2,64,256]{2,1,0:T(8,128)S(1)}, f32[2,64,256]{2,1,0:T(8,128)S(1)}, u32[]{:S(2)}, u32[]{:S(2)}) collective-permute-start(f32[2,64,256]{2,1,0:T(8,128)S(1)} %get-tuple-element.42), channel_id=1, source_target_pairs={{0,12},{2,14},{4,8},{6,10},{8,4},{10,6},{12,0},{14,2},{1,13},{3,15... | collective-permute-start | bytes 393224 | tf_op jit(solution)/shard_map/ppermute | solution.py:465
  31.3 0.0 collective-permute-done.6.refs_6_
  31.3 0.0 collective-permute-start.1
  31.3 0.0 collective-permute-done.5.refs_5_
  31.3 2.0 %collective-permute-start = (f32[2,64,256]{2,1,0:T(8,128)S(1)}, f32[2,64,256]{2,1,0:T(8,128)S(1)}, u32[]{:S(2)}, u32[]{:S(2)}) collective-permute-start(f32[2,64,256]{2,1,0:T(8,128)S(1)} %get-tuple-element.44), channel_id=1, source_target_pairs={{0,2},{2,0},{4,6},{6,4},{8,10},{10,8},{12,14},{14,12},{1,3},{3,1},... | collective-permute-start | bytes 393224 | tf_op jit(solution)/shard_map/ppermute | solution.py:465
  33.3 11.7 %collective-permute-done.4.refs_4_ = f32[2,64,256]{2,1,0:T(8,128)S(1)} collective-permute-done((f32[2,64,256]{2,1,0:T(8,128)S(1)}, f32[2,64,256]{2,1,0:T(8,128)S(1)}, u32[]{:S(2)}, u32[]{:S(2)}) %collective-permute-start.4) | collective-permute-done | bytes 131104 | tf_op jit(solution)/shard_map/ppermute | solution.py:465
  45.0 3.6 %collective-permute-done.3.refs_3_ = f32[2,64,256]{2,1,0:T(8,128)S(1)} collective-permute-done((f32[2,64,256]{2,1,0:T(8,128)S(1)}, f32[2,64,256]{2,1,0:T(8,128)S(1)}, u32[]{:S(2)}, u32[]{:S(2)}) %collective-permute-start.3) | collective-permute-done | bytes 131104 | tf_op jit(solution)/shard_map/ppermute | solution.py:465
  48.6 0.0 collective-permute-done.2.refs_2_
  48.6 0.0 collective-permute-done.1.refs_1_
  48.6 0.0 collective-permute-done.refs_0_
  48.6 1.1 %prior_products.1 = (f32[16,64,256]{2,1,0:T(8,128)S(1)}, f32[64,256]{1,0:T(8,128)S(1)}, f32[8,128]{1,0:T(8,128)S(1)}) custom-call(f32[2,64,256]{2,1,0:T(8,128)S(1)} %collective-permute-done.refs_0_, f32[2,64,256]{2,1,0:T(8,128)S(1)} %collective-permute-done.1.refs_1_, f32[2,64,256]{2,1,0:T(8,128)S(1)} %collective-permute-done.2.refs_2_, ...), custom_call_target="tpu_custom_call" | custom-call | tf_op jit(solution)/shard_map/prior_products/pallas_call | solution.py:286
  49.7 0.0 all-to-all-done
  49.7 0.1 reshape.48
  50.0 0.2 convolution_multiply_fusion
  50.2 0.1 select_maximum_fusion.data_ref
  50.4 0.0 copy-start.5
  50.4 13.2 %all_to_all.10.sums_ref = f32[16,8,128]{2,1,0:T(8,128)S(1)} all-to-all(f32[16,8,128]{2,1,0:T(8,128)S(1)} %send_products.1), channel_id=1, replica_groups=mesh['grp'=2,'mem'=8,'slab'=2] {'mem','slab'}, dimensions={0} | all-to-all | bytes 131072 | tf_op jit(solution)/shard_map/all_to_all | solution.py:475
  63.5 2.2 %mix_update.1 = (f32[2,64,256]{2,1,0:T(8,128)S(1)}, f32[2,64,256]{2,1,0:T(8,128)S(1)}, f32[2,64,256]{2,1,0:T(8,128)S(1)}, f32[2,64,256]{2,1,0:T(8,128)S(1)}, f32...) custom-call(f32[16,8,128]{2,1,0:T(8,128)S(1)} %all_to_all.10.sums_re, ...), custom_call_target="tpu_custom_call" | custom-call | tf_op jit(solution)/shard_map/mix_update/pallas_call | solution.py:381
  65.8 0.2 collective-permute-start.10
  66.0 1.9 %collective-permute-start.11 = (f32[2,64,256]{2,1,0:T(8,128)S(1)}, f32[2,64,256]{2,1,0:T(8,128)S(1)}, u32[]{:S(2)}, u32[]{:S(2)}) collective-permute-start(f32[2,64,256]{2,1,0:T(8,128)S(1)} %get-tuple-element.26), channel_id=1, source_target_pairs={{0,14},{2,12},{4,10},{6,8},{8,6},{10,4},{12,2},{14,0},{1,15},{3,13... | collective-permute-start | bytes 393224 | tf_op jit(solution)/shard_map/ppermute | solution.py:465
  67.8 3.3 %collective-permute-start.12 = (f32[2,64,256]{2,1,0:T(8,128)S(1)}, f32[2,64,256]{2,1,0:T(8,128)S(1)}, u32[]{:S(2)}, u32[]{:S(2)}) collective-permute-start(f32[2,64,256]{2,1,0:T(8,128)S(1)} %get-tuple-element.27), channel_id=1, source_target_pairs={{0,12},{2,14},{4,8},{6,10},{8,4},{10,6},{12,0},{14,2},{1,13},{3,15... | collective-permute-start | bytes 393224 | tf_op jit(solution)/shard_map/ppermute | solution.py:465
  71.1 0.0 collective-permute-start.13
  71.1 2.5 %collective-permute-start.14 = (f32[2,64,256]{2,1,0:T(8,128)S(1)}, f32[2,64,256]{2,1,0:T(8,128)S(1)}, u32[]{:S(2)}, u32[]{:S(2)}) collective-permute-start(f32[2,64,256]{2,1,0:T(8,128)S(1)} %get-tuple-element.29), channel_id=1, source_target_pairs={{0,8},{2,10},{4,12},{6,14},{8,0},{10,2},{12,4},{14,6},{1,9},{3,11}... | collective-permute-start | bytes 393224 | tf_op jit(solution)/shard_map/ppermute | solution.py:465
  73.6 0.0 collective-permute-done.10.refs_0_
  73.6 0.0 collective-permute-start.15
  73.6 1.5 %collective-permute-done.11.refs_1_ = f32[2,64,256]{2,1,0:T(8,128)S(1)} collective-permute-done((f32[2,64,256]{2,1,0:T(8,128)S(1)}, f32[2,64,256]{2,1,0:T(8,128)S(1)}, u32[]{:S(2)}, u32[]{:S(2)}) %collective-permute-start.11) | collective-permute-done | bytes 131104 | tf_op jit(solution)/shard_map/ppermute | solution.py:465
  75.1 10.1 %collective-permute-start.16 = (f32[2,64,256]{2,1,0:T(8,128)S(1)}, f32[2,64,256]{2,1,0:T(8,128)S(1)}, u32[]{:S(2)}, u32[]{:S(2)}) collective-permute-start(f32[2,64,256]{2,1,0:T(8,128)S(1)} %get-tuple-element.31), channel_id=1, source_target_pairs={{0,4},{2,6},{4,0},{6,2},{8,12},{10,14},{12,8},{14,10},{1,5},{3,7},... | collective-permute-start | bytes 393224 | tf_op jit(solution)/shard_map/ppermute | solution.py:465
  85.2 0.6 constant_dynamic-slice_fusion
  85.7 4.5 %collective-permute-done.13.refs_3_ = f32[2,64,256]{2,1,0:T(8,128)S(1)} collective-permute-done((f32[2,64,256]{2,1,0:T(8,128)S(1)}, f32[2,64,256]{2,1,0:T(8,128)S(1)}, u32[]{:S(2)}, u32[]{:S(2)}) %collective-permute-start.13) | collective-permute-done | bytes 131104 | tf_op jit(solution)/shard_map/ppermute | solution.py:465
  90.3 1.6 %collective-permute-done.14.refs_4_ = f32[2,64,256]{2,1,0:T(8,128)S(1)} collective-permute-done((f32[2,64,256]{2,1,0:T(8,128)S(1)}, f32[2,64,256]{2,1,0:T(8,128)S(1)}, u32[]{:S(2)}, u32[]{:S(2)}) %collective-permute-start.14) | collective-permute-done | bytes 131104 | tf_op jit(solution)/shard_map/ppermute | solution.py:465
  91.9 1.0 %collective-permute-done.16.refs_6_ = f32[2,64,256]{2,1,0:T(8,128)S(1)} collective-permute-done((f32[2,64,256]{2,1,0:T(8,128)S(1)}, f32[2,64,256]{2,1,0:T(8,128)S(1)}, u32[]{:S(2)}, u32[]{:S(2)}) %collective-permute-start.16) | collective-permute-done | bytes 131104 | tf_op jit(solution)/shard_map/ppermute | solution.py:465
  92.9 1.0 %join_blocks.1 = f32[2,512,256]{2,1,0:T(8,128)} custom-call(f32[2,64,256]{2,1,0:T(8,128)S(1)} %collective-permute-done.10.refs_0_, f32[2,64,256]{2,1,0:T(8,128)S(1)} %collective-permute-done.11.refs_1_, f32[2,64,256]{2,1,0:T(8,128)S(1)} %collective-permute-done.12.refs_2_, f32[2,64,256]{2,1,0:T(8,128)S(1)} %collective-permute-done.13.refs_3_, ...), custom_call_target="tpu_custom_call" | custom-call | tf_op jit(solution)/shard_map/join_blocks/pallas_call | solution.py:441
  (22 shorter events, 0.2 us)
Async XLA Ops:
  0.6 8.9 %collective-permute-start.7 = (f32[16,32,256]{2,1,0:T(8,128)}, f32[16,32,256]{2,1,0:T(8,128)S(1)}, u32[]{:S(2)}, u32[]{:S(2)}) collective-permute-start(f32[16,32,256]{2,1,0:T(8,128)} %tracer_ref.1), channel_id=1, source_target_pairs={{0,1},{1,0},{2,3},{3,2},{4,5},{5,4},{6,7},{7,6},{8,9},{9,8},{10,11... | collective-permute-start | bytes 1572872 | tf_op jit(solution)/shard_map/ppermute | solution.py:408
  2.9 6.7 %collective-permute-start.9 = (f32[2,2,32,256]{3,2,1,0:T(8,128)}, f32[2,2,32,256]{3,2,1,0:T(8,128)S(1)}, u32[]{:S(2)}, u32[]{:S(2)}) collective-permute-start(f32[2,2,32,256]{3,2,1,0:T(8,128)} %get-tuple-element.35), channel_id=1, source_target_pairs={{1,0},{0,1},{3,2},{2,3},{5,4},{4,5},{7,6},{6,7},{9,8},{8,9},{11,10... | collective-permute-start | bytes 393224 | tf_op jit(solution)/shard_map/ppermute | solution.py:417
  2.9 6.7 %collective-permute-start.8 = (f32[2,2,32,256]{3,2,1,0:T(8,128)}, f32[2,2,32,256]{3,2,1,0:T(8,128)S(1)}, u32[]{:S(2)}, u32[]{:S(2)}) collective-permute-start(f32[2,2,32,256]{3,2,1,0:T(8,128)} %get-tuple-element.36), channel_id=1, source_target_pairs={{0,1},{1,0},{2,3},{3,2},{4,5},{5,4},{6,7},{7,6},{8,9},{9,8},{10,11... | collective-permute-start | bytes 393224 | tf_op jit(solution)/shard_map/ppermute | solution.py:416
  3.4 6.2 %copy-start = (f32[2,16,32,256]{3,2,1,0:T(8,128)S(1)}, f32[2,16,32,256]{3,2,1,0:T(8,128)}, u32[]{:S(2)}) copy-start(f32[2,16,32,256]{3,2,1,0:T(8,128)} %param_ref.1) | copy-start | bytes 3145732
  3.4 6.2 %copy-start.1 = (f32[16,32,256]{2,1,0:T(8,128)S(1)}, f32[16,32,256]{2,1,0:T(8,128)}, u32[]{:S(2)}) copy-start(f32[16,32,256]{2,1,0:T(8,128)} %tracer_ref.1) | copy-start | bytes 1572868
  5.6 4.0 %copy-start.2 = (s32[2048]{0:T(1024)S(1)}, s32[2048]{0:T(1024)}, u32[]{:S(2)}) copy-start(s32[2048]{0:T(1024)} %param.10) | copy-start | bytes 24580
  5.6 25.7 %collective-permute-start.6 = (f32[2,64,256]{2,1,0:T(8,128)}, f32[2,64,256]{2,1,0:T(8,128)S(1)}, u32[]{:S(2)}, u32[]{:S(2)}) collective-permute-start(f32[2,64,256]{2,1,0:T(8,128)} %get-tuple-element.38), channel_id=1, source_target_pairs={{0,4},{2,6},{4,0},{6,2},{8,12},{10,14},{12,8},{14,10},{1,5},{3,7},... | collective-permute-start | bytes 393224 | tf_op jit(solution)/shard_map/ppermute | solution.py:465
  8.2 23.1 %collective-permute-start.5 = (f32[2,64,256]{2,1,0:T(8,128)}, f32[2,64,256]{2,1,0:T(8,128)S(1)}, u32[]{:S(2)}, u32[]{:S(2)}) collective-permute-start(f32[2,64,256]{2,1,0:T(8,128)} %get-tuple-element.39), channel_id=1, source_target_pairs={{0,6},{2,4},{4,2},{6,0},{8,14},{10,12},{12,10},{14,8},{1,7},{3,5},... | collective-permute-start | bytes 393224 | tf_op jit(solution)/shard_map/ppermute | solution.py:465
  9.5 0.7 copy-start.3
  9.5 0.7 copy-start.4
  18.7 31.0 %all-to-all-start = ((f32[8,32,128]{2,1,0:T(8,128)}), f32[8,32,128]{2,1,0:T(8,128)S(1)}, u32[]{:S(2)}, u32[]{:S(2)}) async-start(f32[8,32,128]{2,1,0:T(8,128)} %get-tuple-element.20), calls=%async_computation | async-start | bytes 262144 | tf_op jit(solution)/shard_map/all_to_all | solution.py:475
  23.6 21.4 %collective-permute-start.4 = (f32[2,64,256]{2,1,0:T(8,128)S(1)}, f32[2,64,256]{2,1,0:T(8,128)S(1)}, u32[]{:S(2)}, u32[]{:S(2)}) collective-permute-start(f32[2,64,256]{2,1,0:T(8,128)S(1)} %get-tuple-element.40), channel_id=1, source_target_pairs={{0,8},{2,10},{4,12},{6,14},{8,0},{10,2},{12,4},{14,6},{1,9},{3,11}... | collective-permute-start | bytes 393224 | tf_op jit(solution)/shard_map/ppermute | solution.py:465
  26.5 22.1 %collective-permute-start.3 = (f32[2,64,256]{2,1,0:T(8,128)S(1)}, f32[2,64,256]{2,1,0:T(8,128)S(1)}, u32[]{:S(2)}, u32[]{:S(2)}) collective-permute-start(f32[2,64,256]{2,1,0:T(8,128)S(1)} %get-tuple-element.41), channel_id=1, source_target_pairs={{0,10},{2,8},{4,14},{6,12},{8,2},{10,0},{12,6},{14,4},{1,11},{3,9}... | collective-permute-start | bytes 393224 | tf_op jit(solution)/shard_map/ppermute | solution.py:465
  28.0 20.6 %collective-permute-start.2 = (f32[2,64,256]{2,1,0:T(8,128)S(1)}, f32[2,64,256]{2,1,0:T(8,128)S(1)}, u32[]{:S(2)}, u32[]{:S(2)}) collective-permute-start(f32[2,64,256]{2,1,0:T(8,128)S(1)} %get-tuple-element.42), channel_id=1, source_target_pairs={{0,12},{2,14},{4,8},{6,10},{8,4},{10,6},{12,0},{14,2},{1,13},{3,15... | collective-permute-start | bytes 393224 | tf_op jit(solution)/shard_map/ppermute | solution.py:465
  31.3 17.3 %collective-permute-start.1 = (f32[2,64,256]{2,1,0:T(8,128)S(1)}, f32[2,64,256]{2,1,0:T(8,128)S(1)}, u32[]{:S(2)}, u32[]{:S(2)}) collective-permute-start(f32[2,64,256]{2,1,0:T(8,128)S(1)} %get-tuple-element.43), channel_id=1, source_target_pairs={{0,14},{2,12},{4,10},{6,8},{8,6},{10,4},{12,2},{14,0},{1,15},{3,13... | collective-permute-start | bytes 393224 | tf_op jit(solution)/shard_map/ppermute | solution.py:465
  31.3 17.3 %collective-permute-start = (f32[2,64,256]{2,1,0:T(8,128)S(1)}, f32[2,64,256]{2,1,0:T(8,128)S(1)}, u32[]{:S(2)}, u32[]{:S(2)}) collective-permute-start(f32[2,64,256]{2,1,0:T(8,128)S(1)} %get-tuple-element.44), channel_id=1, source_target_pairs={{0,2},{2,0},{4,6},{6,4},{8,10},{10,8},{12,14},{14,12},{1,3},{3,1},... | collective-permute-start | bytes 393224 | tf_op jit(solution)/shard_map/ppermute | solution.py:465
  50.4 13.2 %copy-start.5 = (f32[16,16]{1,0:T(8,128)S(1)}, f32[16,16]{1,0:T(8,128)}, u32[]{:S(2)}) copy-start(f32[16,16]{1,0:T(8,128)} %noise_ref.1) | copy-start | bytes 3076
  65.8 7.8 %collective-permute-start.10 = (f32[2,64,256]{2,1,0:T(8,128)S(1)}, f32[2,64,256]{2,1,0:T(8,128)S(1)}, u32[]{:S(2)}, u32[]{:S(2)}) collective-permute-start(f32[2,64,256]{2,1,0:T(8,128)S(1)} %get-tuple-element.25), channel_id=1, source_target_pairs={{0,2},{2,0},{4,6},{6,4},{8,10},{10,8},{12,14},{14,12},{1,3},{3,1},... | collective-permute-start | bytes 393224 | tf_op jit(solution)/shard_map/ppermute | solution.py:465
  66.0 9.1 %collective-permute-start.11 = (f32[2,64,256]{2,1,0:T(8,128)S(1)}, f32[2,64,256]{2,1,0:T(8,128)S(1)}, u32[]{:S(2)}, u32[]{:S(2)}) collective-permute-start(f32[2,64,256]{2,1,0:T(8,128)S(1)} %get-tuple-element.26), channel_id=1, source_target_pairs={{0,14},{2,12},{4,10},{6,8},{8,6},{10,4},{12,2},{14,0},{1,15},{3,13... | collective-permute-start | bytes 393224 | tf_op jit(solution)/shard_map/ppermute | solution.py:465
  67.8 17.9 %collective-permute-start.12 = (f32[2,64,256]{2,1,0:T(8,128)S(1)}, f32[2,64,256]{2,1,0:T(8,128)S(1)}, u32[]{:S(2)}, u32[]{:S(2)}) collective-permute-start(f32[2,64,256]{2,1,0:T(8,128)S(1)} %get-tuple-element.27), channel_id=1, source_target_pairs={{0,12},{2,14},{4,8},{6,10},{8,4},{10,6},{12,0},{14,2},{1,13},{3,15... | collective-permute-start | bytes 393224 | tf_op jit(solution)/shard_map/ppermute | solution.py:465
  71.1 19.1 %collective-permute-start.13 = (f32[2,64,256]{2,1,0:T(8,128)S(1)}, f32[2,64,256]{2,1,0:T(8,128)S(1)}, u32[]{:S(2)}, u32[]{:S(2)}) collective-permute-start(f32[2,64,256]{2,1,0:T(8,128)S(1)} %get-tuple-element.28), channel_id=1, source_target_pairs={{0,10},{2,8},{4,14},{6,12},{8,2},{10,0},{12,6},{14,4},{1,11},{3,9}... | collective-permute-start | bytes 393224 | tf_op jit(solution)/shard_map/ppermute | solution.py:465
  71.1 20.8 %collective-permute-start.14 = (f32[2,64,256]{2,1,0:T(8,128)S(1)}, f32[2,64,256]{2,1,0:T(8,128)S(1)}, u32[]{:S(2)}, u32[]{:S(2)}) collective-permute-start(f32[2,64,256]{2,1,0:T(8,128)S(1)} %get-tuple-element.29), channel_id=1, source_target_pairs={{0,8},{2,10},{4,12},{6,14},{8,0},{10,2},{12,4},{14,6},{1,9},{3,11}... | collective-permute-start | bytes 393224 | tf_op jit(solution)/shard_map/ppermute | solution.py:465
  73.6 18.3 %collective-permute-start.15 = (f32[2,64,256]{2,1,0:T(8,128)S(1)}, f32[2,64,256]{2,1,0:T(8,128)S(1)}, u32[]{:S(2)}, u32[]{:S(2)}) collective-permute-start(f32[2,64,256]{2,1,0:T(8,128)S(1)} %get-tuple-element.30), channel_id=1, source_target_pairs={{0,6},{2,4},{4,2},{6,0},{8,14},{10,12},{12,10},{14,8},{1,7},{3,5},... | collective-permute-start | bytes 393224 | tf_op jit(solution)/shard_map/ppermute | solution.py:465
  75.1 17.8 %collective-permute-start.16 = (f32[2,64,256]{2,1,0:T(8,128)S(1)}, f32[2,64,256]{2,1,0:T(8,128)S(1)}, u32[]{:S(2)}, u32[]{:S(2)}) collective-permute-start(f32[2,64,256]{2,1,0:T(8,128)S(1)} %get-tuple-element.31), channel_id=1, source_target_pairs={{0,4},{2,6},{4,0},{6,2},{8,12},{10,14},{12,8},{14,10},{1,5},{3,7},... | collective-permute-start | bytes 393224 | tf_op jit(solution)/shard_map/ppermute | solution.py:465
where the time goes:
time: 94.4 us; the launch traced here: 93.9 us
  starting transfers between devices  37.5 us (40%)
  waiting for transfers between devices  24 us (25%)
  blocking collectives  13.2 us (14%)
  Pallas kernels  12.9 us (14%)
  local copies, waits for them, and re-layouts  5.25 us (6%)
    ppermute x14, starting transfers between devices, swap(): return lax.ppermute(block, 'mem', [(i, i ^ b) for i in range(count)])  31.5 us
    ppermute x14, waiting for transfers between devices, swap(): return lax.ppermute(block, 'mem', [(i, i ^ b) for i in range(count)])  24 us
    all_to_all x1, blocking collectives, broadcast_exchange(): return lax.all_to_all(load, axes, split_axis=0, concat_axis=0, tiled=True)  13.2 us
    pallas_call x1, Pallas kernels, forward_observe(): pl.pallas_call(forward_kernel, out_shape=(jax.ShapeDtypeStruct((members,...  8.47 us
    all_to_all x1, starting transfers between devices, broadcast_exchange(): return lax.all_to_all(load, axes, split_axis=0, concat_axis=0, tiled=True)  4.88 us
    pallas_call x1, Pallas kernels, mix_call(): pl.pallas_call(functools.partial(mix_kernel, total_cells, order), out_sha...  2.21 us
    dynamic_slice x1, local copies, waits for them, and re-layouts, cut_blocks(): lax.dynamic_slice_in_dim(flat, (me ^ b) * rows, rows, axis=1)  2.2 us
  transfers between devices with their start and end apart: 18, of which 6 were waited for; matrix products, arithmetic and copies ran while one was open for 5% of the time, Pallas kernels for 10%

commit v1 on v0

--- a/solution.py
+++ b/solution.py
@@ -22,7 +22,8 @@
 
 VMEM = pl.BlockSpec(memory_space=pltpu.VMEM)
 SMEM = pl.BlockSpec(memory_space=pltpu.SMEM)
-SMALL = pltpu.CompilerParams(vmem_limit_bytes=20 * 2**20)
+SMALL = pltpu.CompilerParams(vmem_limit_bytes=4 * 2**20)
+LARGE = pltpu.CompilerParams(vmem_limit_bytes=12 * 2**20)
 
 
 def ring(axis):
@@ -98,8 +99,11 @@
     pitch = SUBLANES
     row = lax.broadcasted_iota(jnp.int32, (SUBLANES, columns), 0)
 
-    target_ref[...] = observed_ref[...]
-    weight_ref[...] = variance_ref[...]
+    share = target_ref.shape[0]
+    part = lax.axis_index("mem") if seen_ref.shape[0] > 1 else 0
+    mine = pl.ds(part * share, share)
+    target_ref[...] = observed_ref[mine, :]
+    weight_ref[...] = variance_ref[mine, :]
     for i in range(STEPS):
         ext[i] = below_ref[below_ref.shape[0] - STEPS + i]
         ext[STEPS + width + i] = above_ref[i]
@@ -112,7 +116,8 @@
 
     for m in range(members):
         for i in range(rim):
-            kappa[m, i] = KAPPA_BASE + KAPPA_SWING * jnp.tanh(low_ref[m, i])
+            at = low_ref.shape[1] - rim + i
+            kappa[m, i] = KAPPA_BASE + KAPPA_SWING * jnp.tanh(low_ref[m, at])
             kappa[m, rim + width + i] = KAPPA_BASE + KAPPA_SWING * jnp.tanh(high_ref[m, i])
 
     def step_first(i, flux_low):
@@ -169,14 +174,14 @@
             turned = stage[pl.ds(base + m, LANES, stride=members), :].T
             picked = jnp.sum(jnp.where(wanted, turned, 0.0), axis=0, keepdims=True)
             out_ref[m : m + 1, first : first + LANES] = picked
-            seen_ref[0, m * groups + group : m * groups + group + 1, :] = picked
-    for b in range(1, seen_ref.shape[0]):
-        seen_ref[b] = seen_ref[0]
-
-
-def forward_observe(index, tracer, param, layers, params, observed, variance, copies=1):
+            at = m * share + group % share
+            seen_ref[group // share, at : at + 1, :] = picked
+
+
+def forward_observe(index, tracer, param, layers, params, observed, variance, shares=1):
     members, width, levels, columns = param.shape
     count = index.shape[0]
+    share = count // LANES // shares
     rim = STEPS - 1
     rows = width * levels * (columns // LANES) * SUBLANES
     cell = index - lax.axis_index("slab") * (width * levels * columns)
@@ -184,9 +189,9 @@
         forward_kernel,
         out_shape=(
             jax.ShapeDtypeStruct((members, count), jnp.float32),
-            jax.ShapeDtypeStruct((copies, members * count // LANES, LANES), jnp.float32),
-            jax.ShapeDtypeStruct((count // LANES, LANES), jnp.float32),
-            jax.ShapeDtypeStruct((count // LANES, LANES), jnp.float32),
+            jax.ShapeDtypeStruct((shares, members * share, LANES), jnp.float32),
+            jax.ShapeDtypeStruct((share, LANES), jnp.float32),
+            jax.ShapeDtypeStruct((share, LANES), jnp.float32),
         ),
         in_specs=[SMEM] + [VMEM] * 9,
         out_specs=(VMEM,) * 4,
@@ -201,7 +206,7 @@
         cost_estimate=pl.CostEstimate(
             flops=100 * param.size, bytes_accessed=16 * param.size, transcendentals=param.size
         ),
-        compiler_params=SMALL,
+        compiler_params=LARGE,
         name="forward_observe",
     )(
         lax.shift_right_logical(cell, 7) * SUBLANES,
@@ -321,14 +326,29 @@
     return jnp.pad(wide, ((0, 0), (LANES // 2, LANES // 2 - wide.shape[1])))
 
 
-def mix_kernel(
-    total_cells, order, sums_ref, noise_ref, dev_ref, mean_ref, *refs
-):
+def update_blocks(order, coef_ref, dev_ref, mean_ref, outs):
+    ensemble, rows, columns = dev_ref.shape
+    me = lax.axis_index("mem")
+    for out, b in zip(outs, order):
+        members = out.shape[0]
+        for m in range(members):
+            j = (me ^ b) * members + m
+
+            @pl.loop(0, rows // (2 * SUBLANES))
+            def _(r):
+                at = pl.ds(pl.multiple_of(r * 2 * SUBLANES, 2 * SUBLANES), 2 * SUBLANES)
+                total = mean_ref[at, :]
+                for k in range(ensemble):
+                    scale = jnp.broadcast_to(coef_ref[j, k : k + 1, :], (2 * SUBLANES, LANES))
+                    scale = jnp.concatenate([scale] * (columns // LANES), axis=1)
+                    total = total + scale * dev_ref[k, at, :]
+                out[m, at, :] = total
+
+
+def mix_kernel(total_cells, order, sums_ref, noise_ref, dev_ref, mean_ref, *refs):
     outs = refs[: len(order)]
-    rows_ref, coef = refs[len(order) :]
-    ensemble, rows, columns = dev_ref.shape
-    members = outs[0].shape[0]
-    me = lax.axis_index("mem")
+    rows_ref, coef_ref = refs[len(order) :]
+    ensemble = dev_ref.shape[0]
 
     packed = sums_ref[0]
     for i in range(1, sums_ref.shape[0]):
@@ -357,21 +377,12 @@
         0.0,
     )
     for j in range(ensemble):
-        coef[j] = jnp.broadcast_to(weight[:, j : j + 1], (ensemble, LANES))
-
-    for out, b in zip(outs, order):
-        for m in range(members):
-            j = (me ^ b) * members + m
-
-            @pl.loop(0, rows // (2 * SUBLANES))
-            def _(r):
-                at = pl.ds(pl.multiple_of(r * 2 * SUBLANES, 2 * SUBLANES), 2 * SUBLANES)
-                total = mean_ref[at, :]
-                for k in range(ensemble):
-                    scale = jnp.broadcast_to(coef[j, k : k + 1, :], (2 * SUBLANES, LANES))
-                    scale = jnp.concatenate([scale] * (columns // LANES), axis=1)
-                    total = total + scale * dev_ref[k, at, :]
-                out[m, at, :] = total
+        coef_ref[j] = jnp.broadcast_to(weight[:, j : j + 1], (ensemble, LANES))
+    update_blocks(order, coef_ref, dev_ref, mean_ref, outs)
+
+
+def rest_kernel(order, coef_ref, dev_ref, mean_ref, *outs):
+    update_blocks(order, coef_ref, dev_ref, mean_ref, outs)
 
 
 def mix_call(sums, noise, dev, mean, total_cells, order):
@@ -381,37 +392,64 @@
     result = pl.pallas_call(
         functools.partial(mix_kernel, total_cells, order),
         out_shape=(block,) * len(order)
-        + (jax.ShapeDtypeStruct((ensemble, ensemble), jnp.float32),),
+        + (
+            jax.ShapeDtypeStruct((ensemble, ensemble), jnp.float32),
+            jax.ShapeDtypeStruct((ensemble, ensemble, LANES), jnp.float32),
+        ),
         in_specs=[VMEM] * 4,
-        out_specs=(VMEM,) * (len(order) + 1),
-        scratch_shapes=[pltpu.VMEM((ensemble, ensemble, LANES), jnp.float32)],
+        out_specs=(VMEM,) * (len(order) + 2),
         compiler_params=SMALL,
         name="mix_update",
     )(sums, noise, dev, mean)
-    return result[:-1], result[-1]
-
-
-def cut_blocks(param, owners):
+    return list(result[:-2]), result[-2], result[-1]
+
+
+def rest_call(coef, dev, mean, order):
+    ensemble, rows, columns = dev.shape
+    members = ensemble // lax.axis_size("mem")
+    block = jax.ShapeDtypeStruct((members, rows, columns), jnp.float32)
+    return list(
+        pl.pallas_call(
+            functools.partial(rest_kernel, order),
+            out_shape=(block,) * len(order),
+            in_specs=[VMEM] * 3,
+            out_specs=(VMEM,) * len(order),
+            compiler_params=SMALL,
+            name="rest_update",
+        )(coef, dev, mean)
+    )
+
+
+def send_blocks(param, order):
     members, width, levels, columns = param.shape
+    owners = len(order)
     flat = param.reshape(members, width * levels, columns)
     rows = width * levels // owners
     me = lax.axis_index("mem")
-    return [
-        lax.dynamic_slice_in_dim(flat, (me ^ b) * rows, rows, axis=1) for b in range(owners)
-    ]
+    got = []
+    for b in order:
+        at = (me ^ b) * rows
+        block = lax.dynamic_slice(
+            flat, (0, at, 0), (members, rows, columns), allow_negative_indices=False
+        )
+        flat, block = lax.optimization_barrier((flat, block))
+        if b:
+            block = swap(block, b)
+        got.append(block)
+    return got
 
 
 def slab_rims(tracer, param):
     rim = STEPS - 1
     forward, backward = ring("slab")
     if set(forward) == set(backward):
-        moved = lax.ppermute(tracer, "slab", forward)
-        layers = (moved, moved)
-    else:
-        layers = (
-            lax.ppermute(tracer[-STEPS:], "slab", forward),
-            lax.ppermute(tracer[:STEPS], "slab", backward),
-        )
+        layers = lax.ppermute(tracer, "slab", forward)
+        params = lax.ppermute(param, "slab", forward)
+        return (layers, layers), (params, params)
+    layers = (
+        lax.ppermute(tracer[-STEPS:], "slab", forward),
+        lax.ppermute(tracer[:STEPS], "slab", backward),
+    )
     params = (
         lax.ppermute(param[:, -rim:], "slab", forward),
         lax.ppermute(param[:, :rim], "slab", backward),
@@ -457,7 +495,9 @@
 
 def far_first(owners):
     half = owners // 2
-    return (1,) + tuple(range(owners - 1, half - 1, -1)) + tuple(range(half - 1, 1, -1)) + (0,)
+    far = [half + b for b in range(0, half, 2)] + [half + b for b in range(1, half, 2)]
+    near = list(range(2, half)) + ([1] if half > 1 else [])
+    return tuple(far + near) + (0,)
 
 
 def swap(block, b):
@@ -484,13 +524,9 @@
     total_cells = slab_width * levels * columns * lax.axis_size("slab")
 
     slabs = lax.axis_size("slab")
-    blocks = cut_blocks(parameter_field, owners)
     order = far_first(owners)
     layers, params = slab_rims(initial_tracer, parameter_field)
-    near = []
-    for b in order[:-1]:
-        near.append(swap(blocks[b], b))
-    near.append(blocks[0])
+    near = send_blocks(parameter_field, order)
     predicted, seen, target, spread = forward_observe(
         observation_index,
         initial_tracer,
@@ -505,10 +541,14 @@
     data_part = data_products(values, target.reshape(-1), spread.reshape(-1))
 
     dev, mean, prior_part = gram_call(near, order)
-    load = send_call(prior_part, pack_products(data_part / owners), owners * slabs)
+    load = send_call(prior_part, pack_products(data_part), owners * slabs)
     sums = broadcast_exchange(load, ("mem", "slab"))
-    sent, mixing = mix_call(sums, noise, dev, mean, total_cells, order)
-    back = [swap(block, b) for b, block in zip(order[:-1], sent)] + [sent[-1]]
+    far = owners // 2
+    sent, mixing, coef = mix_call(sums, noise, dev, mean, total_cells, order[:far])
+    sent += rest_call(coef, dev, mean, order[far:])
+    back = []
+    for b, block in zip(order, sent):
+        back.append(swap(block, b) if b else block)
     new_field = join_call(back, order).reshape(parameter_field.shape)
     mixing_rows = lax.dynamic_slice_in_dim(
         mixing, lax.axis_index("mem") * members_here, members_here, 0

time: 94.4 us -> 92.4 us (0.979)
  starting transfers between devices: 37.5 us -> 26.2 us
  local copies, waits for them, and re-layouts: 5.25 us -> 13.4 us
  waiting for transfers between devices: 24 us -> 27.9 us
  blocking collectives: 13.2 us -> 9.48 us
  Pallas kernels: 12.9 us -> 13.9 us
    ppermute x14, starting transfers between devices: 31.5 us -> 20 us  [swap(): return lax.ppermute(block, 'mem', [(i, i ^ b) for i in range(count)])]
    dynamic_slice x1 -> x8, local copies, waits for them, and re-layouts: 2.2 us -> 8.34 us  [send_blocks(): lax.dynamic_slice(flat, (0, at, 0), (members, rows, columns), allow_negat...]
    unnamed x12 -> x25, local copies, waits for them, and re-layouts: 0.67 us -> 4.47 us
    all_to_all x1, blocking collectives: 13.2 us -> 9.48 us  [broadcast_exchange(): return lax.all_to_all(load, axes, split_axis=0, concat_axis=0, tiled=True)]
    all_to_all x1, waiting for transfers between devices: 0.01 us -> 2.26 us  [broadcast_exchange(): return lax.all_to_all(load, axes, split_axis=0, concat_axis=0, tiled=True)]
    slice x1 -> x0, local copies, waits for them, and re-layouts: 1.68 us -> none  [slab_rims(): param[:, :rim]]
    ppermute x14, waiting for transfers between devices: 24 us -> 25.6 us  [swap(): return lax.ppermute(block, 'mem', [(i, i ^ b) for i in range(count)])]
    pallas_call x1, Pallas kernels: 1.13 us -> 2.21 us  [gram_call(): pl.pallas_call(functools.partial(gram_kernel, order), out_shape=(jax.Shap...]
  transfers between devices with their start and end apart: 18 -> 17, of which waited for: 6 -> 7; matrix products, arithmetic and copies ran while one was open for 5% -> 10% of each run, Pallas kernels for 10% -> 13%
where the time goes in v1:
time: 92.4 us; the launch traced here: 91.9 us
  waiting for transfers between devices  27.9 us (30%)
  starting transfers between devices  26.2 us (28%)
  Pallas kernels  13.9 us (15%)
  local copies, waits for them, and re-layouts  13.4 us (15%)
  blocking collectives  9.48 us (10%)
    ppermute x14, waiting for transfers between devices, swap(): return lax.ppermute(block, 'mem', [(i, i ^ b) for i in range(count)])  25.6 us
    ppermute x14, starting transfers between devices, swap(): return lax.ppermute(block, 'mem', [(i, i ^ b) for i in range(count)])  20 us
    all_to_all x1, blocking collectives, broadcast_exchange(): return lax.all_to_all(load, axes, split_axis=0, concat_axis=0, tiled=True)  9.48 us
    pallas_call x1, Pallas kernels, forward_observe(): pl.pallas_call(forward_kernel, out_shape=(jax.ShapeDtypeStruct((members,...  8.42 us
    dynamic_slice x8, local copies, waits for them, and re-layouts, send_blocks(): lax.dynamic_slice(flat, (0, at, 0), (members, rows, columns), allow_negat...  8.34 us
    all_to_all x1, starting transfers between devices, broadcast_exchange(): return lax.all_to_all(load, axes, split_axis=0, concat_axis=0, tiled=True)  5.54 us
    unnamed x25, local copies, waits for them, and re-layouts  4.47 us
    all_to_all x1, waiting for transfers between devices, broadcast_exchange(): return lax.all_to_all(load, axes, split_axis=0, concat_axis=0, tiled=True)  2.26 us
  transfers between devices with their start and end apart: 17, of which 7 were waited for; matrix products, arithmetic and copies ran while one was open for 10% of the time, Pallas kernels for 13%

profile of v1, /device:TPU:0, one launch (start us, length us, event | category | flops | bytes accessed | tf_op | source)
XLA Modules:
  0.0 91.9 jit_solution(1166272909365935703)
XLA Ops:
  0.6 0.0 copy-start
  0.6 0.6 collective-permute-start.8
  1.2 0.1 collective-permute-start.7
  1.3 1.6 %constant_dynamic-slice_fusion.8 = f32[2,64,256]{2,1,0:T(8,128)} fusion(f32[2,512,256]{2,1,0:T(8,128)} %bitcast.18, s32[]{:T(128)S(6)} %mul.36), kind=kLoop, calls=%fused_computation.15 | loop fusion | bytes 262148 | tf_op jit(solution)/shard_map/dynamic_slice | solution.py:432
  2.8 1.6 %constant_dynamic-slice_fusion.7 = f32[2,64,256]{2,1,0:T(8,128)} fusion(f32[2,512,256]{2,1,0:T(8,128)} %bitcast.19, s32[]{:T(128)S(6)} %mul.37), kind=kLoop, calls=%fused_computation.14 | loop fusion | bytes 262148 | tf_op jit(solution)/shard_map/dynamic_slice | solution.py:432
  4.4 1.6 %constant_dynamic-slice_fusion.6 = f32[2,64,256]{2,1,0:T(8,128)} fusion(f32[2,512,256]{2,1,0:T(8,128)} %bitcast.20, s32[]{:T(128)S(6)} %mul.38), kind=kLoop, calls=%fused_computation.13 | loop fusion | bytes 262148 | tf_op jit(solution)/shard_map/dynamic_slice | solution.py:432
  6.0 1.6 %constant_dynamic-slice_fusion.5 = f32[2,64,256]{2,1,0:T(8,128)} fusion(f32[2,512,256]{2,1,0:T(8,128)} %bitcast.21, s32[]{:T(128)S(6)} %mul.39), kind=kLoop, calls=%fused_computation.12 | loop fusion | bytes 262148 | tf_op jit(solution)/shard_map/dynamic_slice | solution.py:432
  7.6 0.7 constant_dynamic-slice_fusion.4
  8.3 0.7 constant_dynamic-slice_fusion.3
  9.0 0.7 constant_dynamic-slice_fusion.2
  9.6 2.9 %collective-permute-start.6 = (f32[2,64,256]{2,1,0:T(8,128)}, f32[2,64,256]{2,1,0:T(8,128)S(1)}, u32[]{:S(2)}, u32[]{:S(2)}) collective-permute-start(f32[2,64,256]{2,1,0:T(8,128)} %constant_dynamic-slice_fusion.2), channel_id=1, source_target_pairs={{0,2},{2,0},{4,6},{6,4},{8,10},{10,8},{12,14},{14,12},{1,3},{3,1},... | collective-permute-start | bytes 393224 | tf_op jit(solution)/shard_map/ppermute | solution.py:505
  12.5 1.5 %collective-permute-start.5 = (f32[2,64,256]{2,1,0:T(8,128)}, f32[2,64,256]{2,1,0:T(8,128)S(1)}, u32[]{:S(2)}, u32[]{:S(2)}) collective-permute-start(f32[2,64,256]{2,1,0:T(8,128)} %constant_dynamic-slice_fusion.3), channel_id=1, source_target_pairs={{0,6},{2,4},{4,2},{6,0},{8,14},{10,12},{12,10},{14,8},{1,7},{3,5},... | collective-permute-start | bytes 393224 | tf_op jit(solution)/shard_map/ppermute | solution.py:505
  14.1 0.0 collective-permute-start.4
  14.1 4.5 %collective-permute-done.6.refs_6_ = f32[2,64,256]{2,1,0:T(8,128)S(1)} collective-permute-done((f32[2,64,256]{2,1,0:T(8,128)}, f32[2,64,256]{2,1,0:T(8,128)S(1)}, u32[]{:S(2)}, u32[]{:S(2)}) %collective-permute-start.6) | collective-permute-done | bytes 131104 | tf_op jit(solution)/shard_map/ppermute | solution.py:505
  18.6 5.4 %collective-permute-start.3 = (f32[2,64,256]{2,1,0:T(8,128)}, f32[2,64,256]{2,1,0:T(8,128)}, u32[]{:S(2)}, u32[]{:S(2)}) collective-permute-start(f32[2,64,256]{2,1,0:T(8,128)} %constant_dynamic-slice_fusion.5), channel_id=1, source_target_pairs={{0,14},{2,12},{4,10},{6,8},{8,6},{10,4},{12,2},{14,0},{1,15},{3,13... | collective-permute-start | bytes 393224 | tf_op jit(solution)/shard_map/ppermute | solution.py:505
  24.1 1.4 %collective-permute-start.1 = (f32[2,64,256]{2,1,0:T(8,128)}, f32[2,64,256]{2,1,0:T(8,128)}, u32[]{:S(2)}, u32[]{:S(2)}) collective-permute-start(f32[2,64,256]{2,1,0:T(8,128)} %constant_dynamic-slice_fusion.7), channel_id=1, source_target_pairs={{0,12},{2,14},{4,8},{6,10},{8,4},{10,6},{12,0},{14,2},{1,13},{3,15... | collective-permute-start | bytes 393224 | tf_op jit(solution)/shard_map/ppermute | solution.py:505
  25.5 1.1 %collective-permute-start = (f32[2,64,256]{2,1,0:T(8,128)}, f32[2,64,256]{2,1,0:T(8,128)}, u32[]{:S(2)}, u32[]{:S(2)}) collective-permute-start(f32[2,64,256]{2,1,0:T(8,128)} %constant_dynamic-slice_fusion.8), channel_id=1, source_target_pairs={{0,8},{2,10},{4,12},{6,14},{8,0},{10,2},{12,4},{14,6},{1,9},{3,11}... | collective-permute-start | bytes 393224 | tf_op jit(solution)/shard_map/ppermute | solution.py:505
  26.6 0.0 copy-start.4
  26.6 0.7 copy-done.4
  27.3 0.7 copy-done.5
  28.0 8.4 %forward_observe.1 = (f32[2,2048]{1,0:T(2,128)}, f32[8,4,128]{2,1,0:T(4,128)S(1)}, f32[2,128]{1,0:T(2,128)S(1)}, f32[2,128]{1,0:T(2,128)S(1)}) custom-call(s32[2048]{0:T(1024)S(1)} %shift-right-logical_multiply_fusion.line_ref, s32[16,128]{1,0:T(8,128)S(1)} %bitcast.26, f32[16,32,256]{2,1,0:T(8,128)S(1)} %copy-done.1, f32[2,16,32,256]{3,2,1,0:T(8,128)S(1)} %copy-done, ...), custom_call_target="tpu_custom_call" | custom-call | flops 26214400 | bytes 4194304 | tf_op jit(solution)/shard_map/forward_observe/pallas_call | solution.py:188
  36.4 0.6 copy-done.3
  37.0 0.6 copy-done.7
  37.6 0.6 copy-done.9
  38.1 5.5 %all-to-all-start = ((f32[8,4,128]{2,1,0:T(4,128)}), f32[8,4,128]{2,1,0:T(4,128)S(1)}, u32[]{:S(2)}, u32[]{:S(2)}) async-start(f32[8,4,128]{2,1,0:T(4,128)} %copy-done.3), calls=%async_computation | async-start | bytes 32768 | tf_op jit(solution)/shard_map/all_to_all | solution.py:515
  43.7 2.0 %collective-permute-done.refs_0_ = f32[2,64,256]{2,1,0:T(8,128)} collective-permute-done((f32[2,64,256]{2,1,0:T(8,128)}, f32[2,64,256]{2,1,0:T(8,128)}, u32[]{:S(2)}, u32[]{:S(2)}) %collective-permute-start) | collective-permute-done | bytes 131104 | tf_op jit(solution)/shard_map/ppermute | solution.py:505
  45.8 2.2 %prior_products.1 = (f32[16,64,256]{2,1,0:T(8,128)S(1)}, f32[64,256]{1,0:T(8,128)S(1)}, f32[8,128]{1,0:T(8,128)S(1)}) custom-call(f32[2,64,256]{2,1,0:T(8,128)} %collective-permute-done.refs_0_, f32[2,64,256]{2,1,0:T(8,128)} %collective-permute-done.1.refs_1_, f32[2,64,256]{2,1,0:T(8,128)} %collective-permute-done.2.refs_2_, ...), custom_call_target="tpu_custom_call" | custom-call | tf_op jit(solution)/shard_map/prior_products/pallas_call | solution.py:291
  48.0 2.3 %all-to-all-done = f32[8,4,128]{2,1,0:T(4,128)S(1)} async-done(((f32[8,4,128]{2,1,0:T(4,128)}), f32[8,4,128]{2,1,0:T(4,128)S(1)}, u32[]{:S(2)}, u32[]{:S(2)}) %all-to-all-start) | async-done | bytes 16416 | tf_op jit(solution)/shard_map/all_to_all | solution.py:515
  50.3 0.6 copy-done.10
  50.9 0.7 copy-done.8
  51.7 0.1 fusion.2
  51.8 0.1 select_maximum_fusion.data_ref
  51.9 0.0 copy-start.6
  51.9 9.5 %all_to_all.10.sums_ref = f32[16,8,128]{2,1,0:T(8,128)S(1)} all-to-all(f32[16,8,128]{2,1,0:T(8,128)S(1)} %send_products.1), channel_id=1, replica_groups=mesh['grp'=2,'mem'=8,'slab'=2] {'mem','slab'}, dimensions={0} | all-to-all | bytes 131072 | tf_op jit(solution)/shard_map/all_to_all | solution.py:515
  61.4 1.3 %mix_update.1 = (f32[2,64,256]{2,1,0:T(8,128)S(1)}, f32[2,64,256]{2,1,0:T(8,128)S(1)}, f32[2,64,256]{2,1,0:T(8,128)S(1)}, f32[2,64,256]{2,1,0:T(8,128)S(1)}, f32...) custom-call(f32[16,8,128]{2,1,0:T(8,128)S(1)} %all_to_all.10.sums_ref, f32[16,16]{1,0:T(8,128)S(1)} %copy-done.6, ...), custom_call_target="tpu_custom_call" | custom-call | tf_op jit(solution)/shard_map/mix_update/pallas_call | solution.py:392
  62.8 0.3 collective-permute-start.9
  63.0 2.3 %collective-permute-start.10 = (f32[2,64,256]{2,1,0:T(8,128)S(1)}, f32[2,64,256]{2,1,0:T(8,128)S(1)}, u32[]{:S(2)}, u32[]{:S(2)}) collective-permute-start(f32[2,64,256]{2,1,0:T(8,128)S(1)} %get-tuple-element.57), channel_id=1, source_target_pairs={{0,12},{2,14},{4,8},{6,10},{8,4},{10,6},{12,0},{14,2},{1,13},{3,15... | collective-permute-start | bytes 393224 | tf_op jit(solution)/shard_map/ppermute | solution.py:505
  65.3 0.9 rest_update.1
  66.2 0.2 collective-permute-start.11
  66.4 4.1 %collective-permute-start.12 = (f32[2,64,256]{2,1,0:T(8,128)S(1)}, f32[2,64,256]{2,1,0:T(8,128)S(1)}, u32[]{:S(2)}, u32[]{:S(2)}) collective-permute-start(f32[2,64,256]{2,1,0:T(8,128)S(1)} %get-tuple-element.59), channel_id=1, source_target_pairs={{0,14},{2,12},{4,10},{6,8},{8,6},{10,4},{12,2},{14,0},{1,15},{3,13... | collective-permute-start | bytes 393224 | tf_op jit(solution)/shard_map/ppermute | solution.py:505
  70.5 0.1 collective-permute-start.13
  70.6 9.5 %collective-permute-done.9.refs_0_ = f32[2,64,256]{2,1,0:T(8,128)S(1)} collective-permute-done((f32[2,64,256]{2,1,0:T(8,128)S(1)}, f32[2,64,256]{2,1,0:T(8,128)S(1)}, u32[]{:S(2)}, u32[]{:S(2)}) %collective-permute-start.9) | collective-permute-done | bytes 131104 | tf_op jit(solution)/shard_map/ppermute | solution.py:505
  80.2 0.6 collective-permute-start.15
  80.8 0.6 constant_dynamic-slice_fusion
  81.4 4.6 %collective-permute-done.11.refs_2_ = f32[2,64,256]{2,1,0:T(8,128)S(1)} collective-permute-done((f32[2,64,256]{2,1,0:T(8,128)S(1)}, f32[2,64,256]{2,1,0:T(8,128)S(1)}, u32[]{:S(2)}, u32[]{:S(2)}) %collective-permute-start.11) | collective-permute-done | bytes 131104 | tf_op jit(solution)/shard_map/ppermute | solution.py:505
  86.0 2.6 %collective-permute-done.14.refs_5_ = f32[2,64,256]{2,1,0:T(8,128)S(1)} collective-permute-done((f32[2,64,256]{2,1,0:T(8,128)S(1)}, f32[2,64,256]{2,1,0:T(8,128)S(1)}, u32[]{:S(2)}, u32[]{:S(2)}) %collective-permute-start.14) | collective-permute-done | bytes 131104 | tf_op jit(solution)/shard_map/ppermute | solution.py:505
  88.6 2.3 %collective-permute-done.15.refs_6_ = f32[2,64,256]{2,1,0:T(8,128)S(1)} collective-permute-done((f32[2,64,256]{2,1,0:T(8,128)S(1)}, f32[2,64,256]{2,1,0:T(8,128)S(1)}, u32[]{:S(2)}, u32[]{:S(2)}) %collective-permute-start.15) | collective-permute-done | bytes 131104 | tf_op jit(solution)/shard_map/ppermute | solution.py:505
  90.9 1.0 %join_blocks.1 = f32[2,512,256]{2,1,0:T(8,128)} custom-call(f32[2,64,256]{2,1,0:T(8,128)S(1)} %collective-permute-done.9.refs_0_, f32[2,64,256]{2,1,0:T(8,128)S(1)} %collective-permute-done.10.refs_1_, f32[2,64,256]{2,1,0:T(8,128)S(1)} %collective-permute-done.11.refs_2_, f32[2,64,256]{2,1,0:T(8,128)S(1)} %collective-permute-done.12.refs_3_, ...), custom_call_target="tpu_custom_call" | custom-call | tf_op jit(solution)/shard_map/join_blocks/pallas_call | solution.py:479
  (40 shorter events, 0.2 us)
Async XLA Ops:
  0.6 7.0 %copy-start = (f32[2,16,32,256]{3,2,1,0:T(8,128)S(1)}, f32[2,16,32,256]{3,2,1,0:T(8,128)}, u32[]{:S(2)}) copy-start(f32[2,16,32,256]{3,2,1,0:T(8,128)} %param_ref.1) | copy-start | bytes 3145732
  0.6 24.8 %collective-permute-start.8 = (f32[2,16,32,256]{3,2,1,0:T(8,128)}, f32[2,16,32,256]{3,2,1,0:T(8,128)S(1)}, u32[]{:S(2)}, u32[]{:S(2)}) collective-permute-start(f32[2,16,32,256]{3,2,1,0:T(8,128)} %param_ref.1), channel_id=1, source_target_pairs={{0,1},{1,0},{2,3},{3,2},{4,5},{5,4},{6,7},{7,6},{8,9},{9,8},{10,11... | collective-permute-start | bytes 3145736 | tf_op jit(solution)/shard_map/ppermute | solution.py:447
  1.2 22.9 %collective-permute-start.7 = (f32[16,32,256]{2,1,0:T(8,128)}, f32[16,32,256]{2,1,0:T(8,128)S(1)}, u32[]{:S(2)}, u32[]{:S(2)}) collective-permute-start(f32[16,32,256]{2,1,0:T(8,128)} %tracer_ref.1), channel_id=1, source_target_pairs={{0,1},{1,0},{2,3},{3,2},{4,5},{5,4},{6,7},{7,6},{8,9},{9,8},{10,11... | collective-permute-start | bytes 1572872 | tf_op jit(solution)/shard_map/ppermute | solution.py:446
  6.0 20.6 %copy-start.1 = (f32[16,32,256]{2,1,0:T(8,128)S(1)}, f32[16,32,256]{2,1,0:T(8,128)}, u32[]{:S(2)}) copy-start(f32[16,32,256]{2,1,0:T(8,128)} %tracer_ref.1) | copy-start | bytes 1572868
  8.9 17.6 %copy-start.2 = (s32[2048]{0:T(1024)S(1)}, s32[2048]{0:T(1024)}, u32[]{:S(2)}) copy-start(s32[2048]{0:T(1024)} %param.10) | copy-start | bytes 24580
  9.6 9.0 %collective-permute-start.6 = (f32[2,64,256]{2,1,0:T(8,128)}, f32[2,64,256]{2,1,0:T(8,128)S(1)}, u32[]{:S(2)}, u32[]{:S(2)}) collective-permute-start(f32[2,64,256]{2,1,0:T(8,128)} %constant_dynamic-slice_fusion.2), channel_id=1, source_target_pairs={{0,2},{2,0},{4,6},{6,4},{8,10},{10,8},{12,14},{14,12},{1,3},{3,1},... | collective-permute-start | bytes 393224 | tf_op jit(solution)/shard_map/ppermute | solution.py:505
  12.5 11.5 %collective-permute-start.5 = (f32[2,64,256]{2,1,0:T(8,128)}, f32[2,64,256]{2,1,0:T(8,128)S(1)}, u32[]{:S(2)}, u32[]{:S(2)}) collective-permute-start(f32[2,64,256]{2,1,0:T(8,128)} %constant_dynamic-slice_fusion.3), channel_id=1, source_target_pairs={{0,6},{2,4},{4,2},{6,0},{8,14},{10,12},{12,10},{14,8},{1,7},{3,5},... | collective-permute-start | bytes 393224 | tf_op jit(solution)/shard_map/ppermute | solution.py:505
  14.1 29.6 %collective-permute-start.4 = (f32[2,64,256]{2,1,0:T(8,128)}, f32[2,64,256]{2,1,0:T(8,128)S(1)}, u32[]{:S(2)}, u32[]{:S(2)}) collective-permute-start(f32[2,64,256]{2,1,0:T(8,128)} %constant_dynamic-slice_fusion.4), channel_id=1, source_target_pairs={{0,4},{2,6},{4,0},{6,2},{8,12},{10,14},{12,8},{14,10},{1,5},{3,7},... | collective-permute-start | bytes 393224 | tf_op jit(solution)/shard_map/ppermute | solution.py:505
  18.6 25.0 %collective-permute-start.3 = (f32[2,64,256]{2,1,0:T(8,128)}, f32[2,64,256]{2,1,0:T(8,128)}, u32[]{:S(2)}, u32[]{:S(2)}) collective-permute-start(f32[2,64,256]{2,1,0:T(8,128)} %constant_dynamic-slice_fusion.5), channel_id=1, source_target_pairs={{0,14},{2,12},{4,10},{6,8},{8,6},{10,4},{12,2},{14,0},{1,15},{3,13... | collective-permute-start | bytes 393224 | tf_op jit(solution)/shard_map/ppermute | solution.py:505
  24.1 19.6 %collective-permute-start.2 = (f32[2,64,256]{2,1,0:T(8,128)}, f32[2,64,256]{2,1,0:T(8,128)}, u32[]{:S(2)}, u32[]{:S(2)}) collective-permute-start(f32[2,64,256]{2,1,0:T(8,128)} %constant_dynamic-slice_fusion.6), channel_id=1, source_target_pairs={{0,10},{2,8},{4,14},{6,12},{8,2},{10,0},{12,6},{14,4},{1,11},{3,9}... | collective-permute-start | bytes 393224 | tf_op jit(solution)/shard_map/ppermute | solution.py:505
  24.1 19.6 %collective-permute-start.1 = (f32[2,64,256]{2,1,0:T(8,128)}, f32[2,64,256]{2,1,0:T(8,128)}, u32[]{:S(2)}, u32[]{:S(2)}) collective-permute-start(f32[2,64,256]{2,1,0:T(8,128)} %constant_dynamic-slice_fusion.7), channel_id=1, source_target_pairs={{0,12},{2,14},{4,8},{6,10},{8,4},{10,6},{12,0},{14,2},{1,13},{3,15... | collective-permute-start | bytes 393224 | tf_op jit(solution)/shard_map/ppermute | solution.py:505
  25.5 20.3 %collective-permute-start = (f32[2,64,256]{2,1,0:T(8,128)}, f32[2,64,256]{2,1,0:T(8,128)}, u32[]{:S(2)}, u32[]{:S(2)}) collective-permute-start(f32[2,64,256]{2,1,0:T(8,128)} %constant_dynamic-slice_fusion.8), channel_id=1, source_target_pairs={{0,8},{2,10},{4,12},{6,14},{8,0},{10,2},{12,4},{14,6},{1,9},{3,11}... | collective-permute-start | bytes 393224 | tf_op jit(solution)/shard_map/ppermute | solution.py:505
  26.6 0.7 copy-start.4
  27.3 0.7 copy-start.5
  36.4 0.6 copy-start.3
  37.0 0.6 copy-start.7
  37.6 0.6 copy-start.9
  38.1 12.1 %all-to-all-start = ((f32[8,4,128]{2,1,0:T(4,128)}), f32[8,4,128]{2,1,0:T(4,128)S(1)}, u32[]{:S(2)}, u32[]{:S(2)}) async-start(f32[8,4,128]{2,1,0:T(4,128)} %copy-done.3), calls=%async_computation | async-start | bytes 32768 | tf_op jit(solution)/shard_map/all_to_all | solution.py:515
  50.3 0.7 copy-start.10
  50.9 0.7 copy-start.8
  51.9 9.5 %copy-start.6 = (f32[16,16]{1,0:T(8,128)S(1)}, f32[16,16]{1,0:T(8,128)}, u32[]{:S(2)}) copy-start(f32[16,16]{1,0:T(8,128)} %noise_ref.1) | copy-start | bytes 3076
  62.8 17.4 %collective-permute-start.9 = (f32[2,64,256]{2,1,0:T(8,128)S(1)}, f32[2,64,256]{2,1,0:T(8,128)S(1)}, u32[]{:S(2)}, u32[]{:S(2)}) collective-permute-start(f32[2,64,256]{2,1,0:T(8,128)S(1)} %get-tuple-element.56), channel_id=1, source_target_pairs={{0,8},{2,10},{4,12},{6,14},{8,0},{10,2},{12,4},{14,6},{1,9},{3,11}... | collective-permute-start | bytes 393224 | tf_op jit(solution)/shard_map/ppermute | solution.py:505
  63.0 17.1 %collective-permute-start.10 = (f32[2,64,256]{2,1,0:T(8,128)S(1)}, f32[2,64,256]{2,1,0:T(8,128)S(1)}, u32[]{:S(2)}, u32[]{:S(2)}) collective-permute-start(f32[2,64,256]{2,1,0:T(8,128)S(1)} %get-tuple-element.57), channel_id=1, source_target_pairs={{0,12},{2,14},{4,8},{6,10},{8,4},{10,6},{12,0},{14,2},{1,13},{3,15... | collective-permute-start | bytes 393224 | tf_op jit(solution)/shard_map/ppermute | solution.py:505
  66.2 19.8 %collective-permute-start.11 = (f32[2,64,256]{2,1,0:T(8,128)S(1)}, f32[2,64,256]{2,1,0:T(8,128)S(1)}, u32[]{:S(2)}, u32[]{:S(2)}) collective-permute-start(f32[2,64,256]{2,1,0:T(8,128)S(1)} %get-tuple-element.58), channel_id=1, source_target_pairs={{0,10},{2,8},{4,14},{6,12},{8,2},{10,0},{12,6},{14,4},{1,11},{3,9}... | collective-permute-start | bytes 393224 | tf_op jit(solution)/shard_map/ppermute | solution.py:505
  66.4 19.6 %collective-permute-start.12 = (f32[2,64,256]{2,1,0:T(8,128)S(1)}, f32[2,64,256]{2,1,0:T(8,128)S(1)}, u32[]{:S(2)}, u32[]{:S(2)}) collective-permute-start(f32[2,64,256]{2,1,0:T(8,128)S(1)} %get-tuple-element.59), channel_id=1, source_target_pairs={{0,14},{2,12},{4,10},{6,8},{8,6},{10,4},{12,2},{14,0},{1,15},{3,13... | collective-permute-start | bytes 393224 | tf_op jit(solution)/shard_map/ppermute | solution.py:505
  70.5 15.5 %collective-permute-start.13 = (f32[2,64,256]{2,1,0:T(8,128)S(1)}, f32[2,64,256]{2,1,0:T(8,128)S(1)}, u32[]{:S(2)}, u32[]{:S(2)}) collective-permute-start(f32[2,64,256]{2,1,0:T(8,128)S(1)} %get-tuple-element.61), channel_id=1, source_target_pairs={{0,4},{2,6},{4,0},{6,2},{8,12},{10,14},{12,8},{14,10},{1,5},{3,7},... | collective-permute-start | bytes 393224 | tf_op jit(solution)/shard_map/ppermute | solution.py:505
  80.2 8.4 %collective-permute-start.14 = (f32[2,64,256]{2,1,0:T(8,128)S(1)}, f32[2,64,256]{2,1,0:T(8,128)S(1)}, u32[]{:S(2)}, u32[]{:S(2)}) collective-permute-start(f32[2,64,256]{2,1,0:T(8,128)S(1)} %get-tuple-element.62), channel_id=1, source_target_pairs={{0,6},{2,4},{4,2},{6,0},{8,14},{10,12},{12,10},{14,8},{1,7},{3,5},... | collective-permute-start | bytes 393224 | tf_op jit(solution)/shard_map/ppermute | solution.py:505
  80.2 10.7 %collective-permute-start.15 = (f32[2,64,256]{2,1,0:T(8,128)S(1)}, f32[2,64,256]{2,1,0:T(8,128)S(1)}, u32[]{:S(2)}, u32[]{:S(2)}) collective-permute-start(f32[2,64,256]{2,1,0:T(8,128)S(1)} %get-tuple-element.63), channel_id=1, source_target_pairs={{0,2},{2,0},{4,6},{6,4},{8,10},{10,8},{12,14},{14,12},{1,3},{3,1},... | collective-permute-start | bytes 393224 | tf_op jit(solution)/shard_map/ppermute | solution.py:505
